TPU v7x, 512 devices: a whole 4x8x8 slice. The times are simulated.
512 devices in a mesh: prow: 16 (over z_lo, x, core), pcol: 32 (over y, z_hi).
Axes of the slice: x: 4, y: 8, z: 8 (z_hi: 4, z_lo: 2; z = z_hi * 2 + z_lo), core: 2. Of those that a mesh axis runs over, the one named last changes fastest.
Arguments:
- matrix: float32 [6, 16, 128, 3, 32, 128], P(None, 'prow', None, None, 'pcol'), may hold values from -1 to 40, as said below
- row_codes: int32 [6, 16, 128], P(None, 'prow'), may hold values from 1 to 8
- col_codes: int32 [3, 32, 128], P(None, 'pcol'), may hold values from 1 to 8
- fault_tiles: int32 [96, 2], replicated, may hold values from 0 to 95, as said below
- fault_cells: int32 [96, 2], replicated, may hold values from 0 to 127
- fault_bits: int32 [96], replicated, may hold values from 1 to 2
Outputs:
- factored: float32 [6, 16, 128, 3, 32, 128], P(None, 'prow', None, None, 'pcol')
- col_check: float32 [3, 32, 128], P(None, 'pcol')
- row_check: float32 [6, 16, 128], P(None, 'prow')
- col_flags: float32 [3, 32], P(None, 'pcol')
- row_flags: float32 [6, 16], P(None, 'prow')
Inputs may be any that keep to these rules, and one draw needn't show every extreme that they name: `matrix`: symmetric positive definite. `fault_tiles`: each tile row index appears in exactly one fault, and so does each tile column index.
All inputs are finite; a program needn't handle non-finite values.
Results may differ from a plain program's by a relative error of at most 0.0003.
Values sent between devices are 32-bit elements; how exact they have to be, the bound alone decides.
No kernel may reach another device: no remote copies, remote signals or barrier semaphores. Data moves between devices by JAX's collectives and lax.ppermute only.
A program may use at most 64 MiB of HBM per device.

v0:
```python
import jax
import jax.numpy as jnp
from jax import lax
from jax.sharding import PartitionSpec as P

STEPS = 2


precise = lax.Precision.HIGHEST


def broadcast(block, axis, holder):
    block = jnp.where(lax.axis_index(axis) == holder, block, jnp.zeros_like(block))
    return lax.psum(block, axis)


def factor_diagonal(diagonal):
    factor = jnp.linalg.cholesky(diagonal)
    identity = jnp.eye(diagonal.shape[0], dtype=jnp.float32)
    inverse = jax.scipy.linalg.solve_triangular(factor, identity, lower=True)
    return (factor, inverse)


def form_panel(col_blocks, tile_ids, factor, inverse, step_index):
    product = jnp.einsum("iab,cb->iac", col_blocks, inverse, precision=precise)
    chosen = jnp.where((tile_ids == step_index)[:, None, None], factor[None], 0.0)
    return jnp.where((tile_ids > step_index)[:, None, None], product, chosen)


def update_range(blocks, trailing_rows, trailing_cols):
    update = jnp.einsum("iab,jcb->iajc", trailing_rows, trailing_cols, precision=precise)
    return blocks - update


def local(matrix, row_codes, col_codes, fault_tiles, fault_cells, fault_bits):
    grid_rows = lax.axis_size("prow")
    grid_cols = lax.axis_size("pcol")
    grid_row = lax.axis_index("prow")
    grid_col = lax.axis_index("pcol")
    tile_rows, _, tile_size, tile_cols, _, _ = matrix.shape
    blocks = matrix.reshape(tile_rows, tile_size, tile_cols, tile_size)
    row_weights = row_codes.reshape(tile_rows, tile_size).astype(jnp.float32) * 0.25
    col_weights = col_codes.reshape(tile_cols, tile_size).astype(jnp.float32) * 0.25
    tile_row = jnp.arange(tile_rows, dtype=jnp.int32) * grid_rows + grid_row
    tile_col = jnp.arange(tile_cols, dtype=jnp.int32) * grid_cols + grid_col
    col_check = lax.psum(jnp.einsum("ia,iajc->jc", row_weights, blocks, precision=precise), "prow")
    row_check = lax.psum(jnp.einsum("iajc,jc->ia", blocks, col_weights, precision=precise), "pcol")
    magnitude = jnp.exp2(fault_bits.astype(jnp.float32) - 1.0)
    fault_rows = fault_tiles[:, 0] * tile_size + fault_cells[:, 0]
    fault_cols = fault_tiles[:, 1] * tile_size + fault_cells[:, 1]
    offsets = jnp.arange(tile_size, dtype=jnp.int32)
    local_rows = (tile_row[:, None] * tile_size + offsets[None, :]).reshape(-1)
    local_cols = (tile_col[:, None] * tile_size + offsets[None, :]).reshape(-1)
    hit_rows = (fault_rows[:, None] == local_rows[None, :]).astype(jnp.float32) * magnitude[:, None]
    hit_cols = (fault_cols[:, None] == local_cols[None, :]).astype(jnp.float32)
    faults_added = jnp.dot(hit_rows.T, hit_cols, precision=precise)
    blocks = blocks + faults_added.reshape(tile_rows, tile_size, tile_cols, tile_size)
    picked = (
        jnp.arange(tile_cols, dtype=jnp.int32) * (grid_cols // grid_rows) + grid_col // grid_rows
    )
    owner_row = grid_col % grid_rows

    def factor_panel(blocks, row_check, col_check, step_index):
        root_row = step_index % grid_rows
        root_col = step_index % grid_cols
        local_row = step_index // grid_rows
        local_col = step_index // grid_cols
        diagonal = broadcast(blocks[local_row, :, local_col, :], "prow", root_row)
        factor, inverse = factor_diagonal(diagonal)
        own_rows = form_panel(blocks[:, :, local_col, :], tile_row, factor, inverse, step_index)
        own_check = jnp.dot(inverse, col_check[local_col], precision=precise)
        panel_rows, new_check = (
            broadcast(own_rows, "pcol", root_col),
            broadcast(own_check, "pcol", root_col),
        )
        across = broadcast(jnp.take(panel_rows, picked, axis=0), "prow", owner_row)
        owner_col = grid_col == root_col
        shift_term = jnp.einsum("jab,ja->b", across, col_weights, precision=precise)
        shift_term = shift_term - jnp.where(owner_col, col_weights[local_col], 0.0)
        shift_vector = lax.psum(shift_term, "pcol")
        row_check = row_check - jnp.einsum("iab,b->ia", panel_rows, shift_vector, precision=precise)
        col_update = jnp.einsum("jab,b->ja", across, new_check, precision=precise)
        col_check = col_check - jnp.where((tile_col > step_index)[:, None], col_update, 0.0)
        col_check = col_check.at[local_col].set(
            jnp.where(owner_col, new_check, col_check[local_col])
        )
        trailing_rows = jnp.where((tile_row > step_index)[:, None, None], panel_rows, 0.0)
        trailing_cols = jnp.where((tile_col > step_index)[:, None, None], across, 0.0)
        return (panel_rows, trailing_rows, trailing_cols, row_check, col_check)

    current = factor_panel(blocks, row_check, col_check, 0)
    for step_index in range(STEPS):
        panel_rows, trailing_rows, trailing_cols, row_check, col_check = current
        blocks = update_range(blocks, trailing_rows, trailing_cols)
        if step_index + 1 < STEPS:
            current = factor_panel(blocks, row_check, col_check, step_index + 1)
        settle_blocks = blocks
        settle_local_col = step_index // grid_cols
        previous = settle_blocks[:, :, settle_local_col, :]
        settle_blocks = settle_blocks.at[:, :, settle_local_col, :].set(
            jnp.where(grid_col == step_index % grid_cols, panel_rows, previous)
        )
        cleared = (tile_row == step_index)[:, None, None, None] & (tile_col > step_index)[
            None, None, :, None
        ]
        blocks = jnp.where(cleared, 0.0, settle_blocks)
    col_found = lax.psum(jnp.einsum("ia,iajc->jc", row_weights, blocks, precision=precise), "prow")
    row_found = lax.psum(jnp.einsum("iajc,jc->ia", blocks, col_weights, precision=precise), "pcol")
    col_flags = jnp.max(jnp.abs(col_check - col_found), axis=1)
    row_flags = jnp.max(jnp.abs(row_check - row_found), axis=1)
    return (
        blocks.reshape(matrix.shape),
        col_check.reshape(tile_cols, 1, tile_size),
        row_check.reshape(tile_rows, 1, tile_size),
        col_flags.reshape(tile_cols, 1),
        row_flags.reshape(tile_rows, 1),
    )


def solution(mesh):
    return jax.shard_map(
        local,
        mesh=mesh,
        in_specs=(
            P(None, "prow", None, None, "pcol", None),
            P(None, "prow", None),
            P(None, "pcol", None),
            P(),
            P(),
            P(),
        ),
        out_specs=(
            P(None, "prow", None, None, "pcol", None),
            P(None, "pcol", None),
            P(None, "prow", None),
            P(None, "pcol"),
            P(None, "prow"),
        ),
        check_vma=False,
    )
```

profile of v0, /device:TPU:64, one launch (start us, length us, event | category | flops | bytes accessed | tf_op | source)
XLA Modules:
  0.0 1394.3 jit_solution(15013393687045354452)
XLA Ops:
  9.6 1.3 reshape.353
  12.1 1.7 bitcast_add_fusion
  15.9 119.9 %all-reduce.9.cloned.1.call-done = f32[128,128]{0,1:T(8,128)} async-done(((f32[128,128]{0,1:T(8,128)}), f32[128,128]{0,1:T(8,128)}) %all-reduce.9.cloned.1.call-update) | async-done | bytes 65552 | tf_op jit(solution)/shard_map/psum | solution.py:14
  137.6 11.7 cholesky.44
  150.7 9.8 custom-call.6
  160.9 1.2 fusion.1
  162.9 312.2 %all-reduce.11.cloned.1.call-done = f32[6,128,128]{1,2,0:T(8,128)} async-done(((f32[6,128,128]{1,2,0:T(8,128)}), f32[6,128,128]{1,2,0:T(8,128)}) %all-reduce.11.cloned.1.call-update) | async-done | bytes 393232 | tf_op jit(solution)/shard_map/psum | solution.py:14
  475.1 1.6 gather_fusion
  478.2 119.6 %all-reduce.13.cloned.1.call-done = f32[3,128,128]{1,2,0:T(8,128)} async-done(((f32[3,128,128]{1,2,0:T(8,128)}), f32[3,128,128]{1,2,0:T(8,128)}) %all-reduce.13.cloned.1.call-update) | async-done | bytes 196624 | tf_op jit(solution)/shard_map/psum | solution.py:14
  597.8 2.3 convolution_subtract_fusion.1
  601.0 1.7 convolution_reduce_fusion.1
  602.7 117.1 %all-reduce.15.cloned.1.call-done = f32[128,128]{0,1:T(8,128)} async-done(((f32[128,128]{0,1:T(8,128)}), f32[128,128]{0,1:T(8,128)}) %all-reduce.15.cloned.1.call-update) | async-done | bytes 65552 | tf_op jit(solution)/shard_map/psum | solution.py:14
  721.6 11.7 cholesky.55
  734.6 9.8 custom-call.7
  744.9 1.2 fusion
  747.1 312.0 %all-reduce.17.cloned.1.call-done = f32[6,128,128]{1,2,0:T(8,128)} async-done(((f32[6,128,128]{1,2,0:T(8,128)}), f32[6,128,128]{1,2,0:T(8,128)}) %all-reduce.17.cloned.1.call-update) | async-done | bytes 393232 | tf_op jit(solution)/shard_map/psum | solution.py:14
  1059.1 1.7 gather_fusion.1
  1061.7 120.0 %all-reduce.19.cloned.1.call-done = f32[3,128,128]{1,2,0:T(8,128)} async-done(((f32[3,128,128]{1,2,0:T(8,128)}), f32[3,128,128]{1,2,0:T(8,128)}) %all-reduce.19.cloned.1.call-update) | async-done | bytes 196624 | tf_op jit(solution)/shard_map/psum | solution.py:14
  1181.7 2.2 convolution_subtract_fusion
  1185.4 1.1 convolution_reduce_fusion
  1186.5 30.2 %all-reduce.1 = (f32[3,128]{1,0:T(4,128)S(1)}, f32[3,128]{1,0:T(4,128)S(1)}) all-reduce(f32[3,128]{1,0:T(4,128)S(1)} %bitcast.205, f32[3,128]{1,0:T(4,128)S(1)} %bitcast.206), channel_id=1, replica_groups=mesh['prow'=16,'pcol'=32] {'prow'}, use_global_device_ids=true, to_apply=%region_8.12 | all-reduce | flops 768 | bytes 6144 | tf_op jit(solution)/shard_map/psum | solution.py:46
  1216.8 83.8 %psum.105 = f32[128]{0:T(128)S(1)} all-reduce(f32[128]{0:T(128)S(1)} %fusion.5), channel_id=1, replica_groups=mesh['prow'=16,'pcol'=32] {'pcol'}, use_global_device_ids=true, to_apply=%region_9.13 | all-reduce | flops 128 | bytes 1024 | tf_op jit(solution)/shard_map/psum | solution.py:14
  1301.9 2.6 copy.50
  1304.9 79.1 %all-reduce = (f32[128]{0:T(128)S(1)}, f32[6,128]{1,0:T(8,128)S(1)}, f32[128]{0:T(128)S(1)}, f32[128]{0:T(128)S(1)}, f32[6,128]{1,0:T(8,128)S(1)}) all-reduce(f32[128]{0:T(128)S(1)} %fusion.4, f32[6,128]{1,0:T(8,128)S(1)} %bitcast.203, f32[128]{0:T(128)S(1)} %fusion.6, ...), channel_id=1, replica_groups=mesh['prow'=16,'pcol'=32] {'pcol'}, use_global_device_ids=true, to_apply=%region_10.14 | all-reduce | flops 1920 | bytes 15360 | tf_op jit(solution)/shard_map/psum | solution.py:14
  (135 shorter events, 24.0 us)
Async XLA Ops:
  7.2 128.6 %all-reduce.9.cloned.1.call-start = ((), (), s32[]{:S(2)}) async-start(), calls=%async_computation | async-start | bytes 131072 | tf_op jit(solution)/shard_map/psum | solution.py:14
  14.5 460.6 %all-reduce.11.cloned.1.call-start = ((), (), s32[]{:S(2)}) async-start(), calls=%async_computation.1 | async-start | bytes 786432 | tf_op jit(solution)/shard_map/psum | solution.py:14
  14.6 462.9 %copy-start.18 = (pred[3]{0:T(512)(128)(4,1)}, pred[3]{0:T(512)(128)(4,1)S(1)}, u32[]{:S(2)}) copy-start(pred[3]{0:T(512)(128)(4,1)S(1)} %broadcast_compare_fusion.3) | copy-start | bytes 13
  14.6 148.3 %copy-start.29 = (pred[6]{0:T(512)(128)(4,1)}, pred[6]{0:T(512)(128)(4,1)S(1)}, u32[]{:S(2)}) copy-start(pred[6]{0:T(512)(128)(4,1)S(1)} %get-tuple-element.81) | copy-start | bytes 22
  15.2 462.3 %copy-start.27 = (pred[6]{0:T(512)(128)(4,1)}, pred[6]{0:T(512)(128)(4,1)S(1)}, u32[]{:S(2)}) copy-start(pred[6]{0:T(512)(128)(4,1)S(1)} %get-tuple-element.84) | copy-start | bytes 22
  15.9 460.8 %copy-start.24 = (pred[3]{0:T(512)(128)(4,1)}, pred[3]{0:T(512)(128)(4,1)S(1)}, u32[]{:S(2)}) copy-start(pred[3]{0:T(512)(128)(4,1)S(1)} %compare_and_fusion) | copy-start | bytes 13
  162.1 435.7 %all-reduce.13.cloned.1.call-start = ((), (), s32[]{:S(2)}) async-start(), calls=%async_computation.2 | async-start | bytes 393216 | tf_op jit(solution)/shard_map/psum | solution.py:14
  162.2 315.9 %copy-start.17 = (s32[1024]{0:T(1024)}, s32[1024]{0:T(1024)S(1)}, u32[]{:S(2)}) copy-start(s32[1024]{0:T(1024)S(1)} %pad_clamp_fusion) | copy-start | bytes 12292
  477.4 242.4 %all-reduce.15.cloned.1.call-start = ((), (), s32[]{:S(2)}) async-start(), calls=%async_computation.3 | async-start | bytes 131072 | tf_op jit(solution)/shard_map/psum | solution.py:14
  478.2 122.9 %copy-start.13 = (s32[6,1,128]{2,1,0:T(1,128)S(1)}, s32[6,1,128]{2,1,0:T(1,128)}, u32[]{:S(2)}) copy-start(s32[6,1,128]{2,1,0:T(1,128)} %param.20) | copy-start | bytes 9220
  600.1 144.7 %copy-start.23 = (pred[6]{0:T(512)(128)(4,1)S(1)}, pred[6]{0:T(512)(128)(4,1)}, u32[]{:S(2)}) copy-start(pred[6]{0:T(512)(128)(4,1)} %get-tuple-element.83) | copy-start | bytes 22
  600.1 144.7 %copy-start.28 = (pred[6]{0:T(512)(128)(4,1)S(1)}, pred[6]{0:T(512)(128)(4,1)}, u32[]{:S(2)}) copy-start(pred[6]{0:T(512)(128)(4,1)} %copy-done.27) | copy-start | bytes 22
  600.8 458.3 %all-reduce.17.cloned.1.call-start = ((), (), s32[]{:S(2)}) async-start(), calls=%async_computation.4 | async-start | bytes 786432 | tf_op jit(solution)/shard_map/psum | solution.py:14
  602.7 143.5 %copy-start.5 = (f32[3,128,128]{1,2,0:T(8,128)S(1)}, f32[3,128,128]{1,2,0:T(8,128)}, u32[]{:S(2)}) copy-start(f32[3,128,128]{1,2,0:T(8,128)} %all-reduce.13.cloned.1.call-done) | copy-start | bytes 589828
  744.9 316.0 %copy-start.25 = (pred[3]{0:T(512)(128)(4,1)S(1)}, pred[3]{0:T(512)(128)(4,1)}, u32[]{:S(2)}) copy-start(pred[3]{0:T(512)(128)(4,1)} %copy-done.24) | copy-start | bytes 13
  746.1 315.5 %copy-start.2 = (f32[6,128,128]{1,2,0:T(8,128)S(1)}, f32[6,128,128]{1,2,0:T(8,128)}, u32[]{:S(2)}) copy-start(f32[6,128,128]{1,2,0:T(8,128)} %all-reduce.11.cloned.1.call-done) | copy-start | bytes 1179652
  746.2 435.5 %all-reduce.19.cloned.1.call-start = ((), (), s32[]{:S(2)}) async-start(), calls=%async_computation.5 | async-start | bytes 393216 | tf_op jit(solution)/shard_map/psum | solution.py:14
  747.1 434.6 %copy-start.19 = (pred[3]{0:T(512)(128)(4,1)S(1)}, pred[3]{0:T(512)(128)(4,1)}, u32[]{:S(2)}) copy-start(pred[3]{0:T(512)(128)(4,1)} %copy-done.18) | copy-start | bytes 13
  747.1 434.6 %copy-start.22 = (pred[6,3]{1,0:T(8,128)(4,1)S(1)}, pred[6,3]{1,0:T(8,128)(4,1)}, u32[]{:S(2)}) copy-start(pred[6,3]{1,0:T(8,128)(4,1)} %broadcast_and_fusion) | copy-start | bytes 58
  1059.1 122.6 %copy-start = (f32[6,128,128]{1,2,0:T(8,128)S(1)}, f32[6,128,128]{1,2,0:T(8,128)}, u32[]{:S(2)}) copy-start(f32[6,128,128]{1,2,0:T(8,128)} %all-reduce.17.cloned.1.call-done) | copy-start | bytes 1179652
  1184.9 115.8 %copy-start.6 = (f32[3,128,128]{1,2,0:T(8,128)S(1)}, f32[3,128,128]{1,2,0:T(8,128)}, u32[]{:S(2)}) copy-start(f32[3,128,128]{1,2,0:T(8,128)} %all-reduce.13.cloned.1.call-done) | copy-start | bytes 589828
  1184.9 116.0 %copy-start.21 = (pred[3]{0:T(512)(128)(4,1)S(1)}, pred[3]{0:T(512)(128)(4,1)}, u32[]{:S(2)}) copy-start(pred[3]{0:T(512)(128)(4,1)} %copy-done.20) | copy-start | bytes 13
  1184.9 116.1 %copy-start.11 = (f32[128,128]{1,0:T(8,128)S(1)}, f32[128,128]{1,0:T(8,128)}, u32[]{:S(2)}) copy-start(f32[128,128]{1,0:T(8,128)} %copy-done.10) | copy-start | bytes 196612
  1301.9 83.9 %copy-start.1 = (f32[6,128,128]{1,2,0:T(8,128)S(1)}, f32[6,128,128]{1,2,0:T(8,128)}, u32[]{:S(2)}) copy-start(f32[6,128,128]{1,2,0:T(8,128)} %all-reduce.17.cloned.1.call-done) | copy-start | bytes 1179652
  (12 other events, 133.7 us)
Sparse Core Ops, SparseCore 0:
  14.6 121.1 all-reduce.8
  162.3 312.7 all-reduce.10
  478.6 119.1 all-reduce.12
  601.1 118.6 all-reduce.14
  746.3 312.7 all-reduce.16
  1062.4 119.1 all-reduce.18
where the time goes:
time: 1390 us
  waiting for transfers between devices  1100 us (79%)
  blocking collectives  193 us (14%)
  other arithmetic  57.3 us (4%)
  matrix products  15.1 us (1%)
  between operations  14.7 us (1%)
    psum x6, waiting for transfers between devices, broadcast(): return lax.psum(block, axis)  1100 us
    psum x2, blocking collectives, broadcast(): return lax.psum(block, axis)  163 us
    psum x1, blocking collectives, local(): lax.psum(jnp.einsum('ia,iajc->jc', row_weights, blocks, precision=precise...  30.2 us
  transfers between devices with their start and end apart: 6, of which 6 were waited for; matrix products, arithmetic and copies ran while one was open for 0% of the time, Pallas kernels for 0%

commit v1 on v0

v1 whole, which is shorter than its diff:
```python
import jax
import jax.numpy as jnp
from jax import lax
from jax.sharding import PartitionSpec as P

precise = lax.Precision.HIGHEST


def spread(pieces, axis):
    return lax.all_to_all(pieces, axis, 0, 0, tiled=True)


def collect(piece, axis):
    count = lax.axis_size(axis)
    return spread(jnp.broadcast_to(piece[None], (count, *piece.shape)), axis)


def factor_tile(tile):
    factor = jnp.linalg.cholesky(tile)
    identity = jnp.eye(tile.shape[0], dtype=jnp.float32)
    inverse = jax.scipy.linalg.solve_triangular(factor, identity, lower=True)
    return factor, inverse


def local(matrix, row_codes, col_codes, fault_tiles, fault_cells, fault_bits):
    grid_rows = lax.axis_size("prow")
    grid_cols = lax.axis_size("pcol")
    grid_row = lax.axis_index("prow")
    grid_col = lax.axis_index("pcol")
    tile_rows, _, size, tile_cols, _, _ = matrix.shape
    rows = tile_rows * size
    cols = tile_cols * size
    blocks = matrix.reshape(rows, tile_cols, size)
    row_weights = row_codes.reshape(rows).astype(jnp.float32) * 0.25
    col_weights = col_codes.reshape(tile_cols, size).astype(jnp.float32) * 0.25
    tile_row = jnp.arange(tile_rows, dtype=jnp.int32) * grid_rows + grid_row
    tile_col = jnp.arange(tile_cols, dtype=jnp.int32) * grid_cols + grid_col
    offsets = jnp.arange(size, dtype=jnp.int32)
    own_rows = (tile_row[:, None] * size + offsets).reshape(rows)
    own_cols = (tile_col[:, None] * size + offsets).reshape(cols)

    part = size // grid_rows
    top = spread(blocks[:size].reshape(grid_rows, part * tile_cols, size), "prow")[:2]
    top = collect(top, "prow").reshape(grid_rows, 2, part, tile_cols, size)
    top = top.transpose(1, 0, 2, 3, 4).reshape(2, size, tile_cols, size)

    left = jnp.concatenate([blocks[:, 0, :], top[:, :, 0, :].reshape(2 * size, size)], axis=0)
    count = left.shape[0] // grid_cols
    left = spread(left.reshape(grid_cols, count, size), "pcol")[:2]
    left = collect(left, "pcol").transpose(1, 0, 2, 3).reshape(2, grid_cols * count, size)

    magnitude = jnp.exp2(fault_bits.astype(jnp.float32) - 1.0)
    fault_rows = fault_tiles[:, 0] * size + fault_cells[:, 0]
    fault_cols = fault_tiles[:, 1] * size + fault_cells[:, 1]
    lead = jnp.arange(2 * size, dtype=jnp.int32)

    def hits(marks, places):
        return (marks[:, None] == places[None, :]).astype(jnp.float32)

    panel_rows = jnp.concatenate([own_rows, lead, own_cols])
    hit_rows = hits(fault_rows, panel_rows) * magnitude[:, None]
    hit_lead = hits(fault_cols, lead)
    hit_cols = hits(fault_cols, own_cols)
    added = jnp.einsum("fr,fkc->krc", hit_rows, hit_lead.reshape(-1, 2, size), precision=precise)
    left_faulty = left + added[:, : rows + 2 * size]
    top_faulty = top.transpose(0, 2, 3, 1).reshape(2, cols, size) + added[:, rows + 2 * size :]

    factor0, inverse0 = factor_tile(left_faulty[0, rows : rows + size])
    below = jnp.einsum("ab,cb->ac", left_faulty[0, rows + size :], inverse0, precision=precise)
    square = left_faulty[1, rows + size :] - jnp.einsum("ab,cb->ac", below, below, precision=precise)
    factor1, inverse1 = factor_tile(square)

    panel = jnp.concatenate([left_faulty[:, :rows], top_faulty], axis=1)
    tile_of = jnp.concatenate([jnp.repeat(tile_row, size), jnp.repeat(tile_col, size)])[:, None]
    copies = tile_rows + tile_cols
    panel0 = jnp.einsum("ab,cb->ac", panel[0], inverse0, precision=precise)
    shifted = panel[1] - jnp.einsum("ab,cb->ac", panel0, below, precision=precise)
    panel1 = jnp.einsum("ab,cb->ac", shifted, inverse1, precision=precise)
    panel0 = jnp.where(tile_of > 0, panel0, jnp.tile(factor0, (copies, 1)))
    panel1 = jnp.where(tile_of > 1, panel1, jnp.where(tile_of == 1, jnp.tile(factor1, (copies, 1)), 0.0))
    trailing = jnp.concatenate(
        [jnp.where(tile_of > 0, panel0, 0.0), jnp.where(tile_of > 1, panel1, 0.0)], axis=1
    )
    update = jnp.einsum(
        "ab,jcb->ajc", trailing[:rows], trailing[rows:].reshape(tile_cols, size, 2 * size), precision=precise
    )
    faults_added = jnp.einsum("fr,fjc->rjc", hit_rows[:, :rows], hit_cols.reshape(-1, tile_cols, size), precision=precise)
    result = blocks + faults_added - update
    row_tile = tile_of[:rows, :, None]
    col_tile = tile_col[None, :, None]
    result = jnp.where(col_tile == 0, panel0[:rows, None, :], result)
    result = jnp.where(col_tile == 1, panel1[:rows, None, :], result)
    result = jnp.where((row_tile < 2) & (col_tile > row_tile), 0.0, result)

    col_clean = jnp.einsum("a,ajc->jc", row_weights, blocks, precision=precise)
    col_found = jnp.einsum("a,ajc->jc", row_weights, result, precision=precise)
    col_lead = jnp.einsum("a,kac->kc", row_weights, left[:, :rows], precision=precise)
    col_sums = jnp.concatenate([col_clean, col_found, col_lead])
    row_clean = jnp.einsum("ajc,jc->a", blocks, col_weights, precision=precise)
    row_found = jnp.einsum("ajc,jc->a", result, col_weights, precision=precise)
    flat_weights = col_weights.reshape(cols)
    steps = jnp.arange(2, dtype=jnp.int32)
    own_lead = jnp.where(steps[:, None] == grid_col, col_weights[0][None], 0.0)
    shift = jnp.stack(
        [
            jnp.einsum("a,ab->b", flat_weights, panel0[rows:], precision=precise),
            jnp.einsum("a,ab->b", flat_weights, panel1[rows:], precision=precise),
        ]
    )
    row_sums = jnp.concatenate(
        [row_clean.reshape(tile_rows, size), row_found.reshape(tile_rows, size), shift - own_lead]
    )
    col_sums = jnp.sum(collect(col_sums, "prow").reshape(grid_rows, *col_sums.shape), axis=0)
    row_sums = jnp.sum(collect(row_sums, "pcol").reshape(grid_cols, *row_sums.shape), axis=0)

    head0 = jnp.dot(inverse0, col_sums[2 * tile_cols], precision=precise)
    head1 = jnp.dot(
        inverse1, col_sums[2 * tile_cols + 1] - jnp.dot(below, head0, precision=precise), precision=precise
    )
    taken0 = jnp.dot(panel0[rows:], head0, precision=precise).reshape(tile_cols, size)
    taken1 = jnp.dot(panel1[rows:], head1, precision=precise).reshape(tile_cols, size)
    col_check = col_sums[:tile_cols] - taken0 - taken1
    col_check = jnp.where(tile_col[:, None] == 0, head0[None], col_check)
    col_check = jnp.where(tile_col[:, None] == 1, head1[None], col_check)
    row_taken = jnp.dot(panel0[:rows], row_sums[2 * tile_rows], precision=precise)
    row_taken = row_taken + jnp.dot(panel1[:rows], row_sums[2 * tile_rows + 1], precision=precise)
    row_check = row_sums[:tile_rows] - row_taken.reshape(tile_rows, size)
    col_flags = jnp.max(jnp.abs(col_check - col_sums[tile_cols : 2 * tile_cols]), axis=1)
    row_flags = jnp.max(jnp.abs(row_check - row_sums[tile_rows : 2 * tile_rows]), axis=1)
    return (
        result.reshape(matrix.shape),
        col_check.reshape(tile_cols, 1, size),
        row_check.reshape(tile_rows, 1, size),
        col_flags.reshape(tile_cols, 1),
        row_flags.reshape(tile_rows, 1),
    )


def solution(mesh):
    return jax.shard_map(
        local,
        mesh=mesh,
        in_specs=(
            P(None, "prow", None, None, "pcol", None),
            P(None, "prow", None),
            P(None, "pcol", None),
            P(),
            P(),
            P(),
        ),
        out_specs=(
            P(None, "prow", None, None, "pcol", None),
            P(None, "pcol", None),
            P(None, "prow", None),
            P(None, "pcol"),
            P(None, "prow"),
        ),
        check_vma=False,
    )
```

time: 1390 us -> 219 us (0.16)
  the two profiles are of different devices: /device:TPU:64 before, /device:TPU:8 now
where the time goes in v1:
time: 219 us; the launch traced here: 218 us
  waiting for transfers between devices  71.6 us (33%)
  other arithmetic  56.4 us (26%)
  starting transfers between devices  41.5 us (19%)
  local copies, waits for them, and re-layouts  24.4 us (11%)
  matrix products  22.6 us (10%)
    all_to_all x6, waiting for transfers between devices, spread(): return lax.all_to_all(pieces, axis, 0, 0, tiled=True)  71.6 us
    all_to_all x6, starting transfers between devices, spread(): return lax.all_to_all(pieces, axis, 0, 0, tiled=True)  41.5 us
    another operation x6, other arithmetic, factor_tile(): factor = jnp.linalg.cholesky(tile)  25 us
    another operation x4, other arithmetic, factor_tile(): inverse = jax.scipy.linalg.solve_triangular(factor, identity, lower=True)  21.6 us
    unnamed x62, local copies, waits for them, and re-layouts  6.05 us
    dot_general x1, matrix products, local(): jnp.einsum('ab,jcb->ajc', trailing[:rows], trailing[rows:].reshape(tile_c...  4.65 us
  transfers between devices with their start and end apart: 6, of which 6 were waited for; matrix products, arithmetic and copies ran while one was open for 6% of the time, Pallas kernels for 0%

profile of v1, /device:TPU:8, one launch (start us, length us, event | category | flops | bytes accessed | tf_op | source)
XLA Modules:
  0.0 217.7 jit_solution(9527269415964741472)
XLA Ops:
  0.6 1.8 slice.119
  2.4 6.2 %all-to-all-start = ((f32[16,24,128]{2,1,0:T(8,128)}), f32[16,24,128]{2,1,0:T(8,128)S(1)}, u32[]{:S(2)}, u32[]{:S(2)}) async-start(f32[16,24,128]{2,1,0:T(8,128)} %bitcast.2), calls=%async_computation | async-start | bytes 393216 | tf_op jit(solution)/shard_map/all_to_all | solution.py:10
  8.8 7.2 %all-to-all-done = f32[16,24,128]{2,1,0:T(8,128)S(1)} async-done(((f32[16,24,128]{2,1,0:T(8,128)}), f32[16,24,128]{2,1,0:T(8,128)S(1)}, u32[]{:S(2)}, u32[]{:S(2)}) %all-to-all-start) | async-done | bytes 196640 | tf_op jit(solution)/shard_map/all_to_all | solution.py:10
  16.8 3.6 %all-to-all-start.1 = ((f32[16,2,24,128]{3,2,1,0:T(8,128)}), f32[16,2,24,128]{3,2,1,0:T(8,128)S(1)}, u32[]{:S(2)}, u32[]{:S(2)}) async-start(f32[16,2,24,128]{3,2,1,0:T(8,128)} %broadcast_in_dim.179), calls=%async_computation.1 | async-start | bytes 786432 | tf_op jit(solution)/shard_map/all_to_all | solution.py:10
  22.4 7.4 %all-to-all-done.1 = f32[16,2,24,128]{3,2,1,0:T(8,128)S(1)} async-done(((f32[16,2,24,128]{3,2,1,0:T(8,128)}), f32[16,2,24,128]{3,2,1,0:T(8,128)S(1)}, u32[]{:S(2)}, u32[]{:S(2)}) %all-to-all-start.1) | async-done | bytes 393248 | tf_op jit(solution)/shard_map/all_to_all | solution.py:10
  30.9 15.3 %all-to-all-start.2 = ((f32[32,32,128]{2,1,0:T(8,128)}), f32[32,32,128]{2,1,0:T(8,128)S(1)}, u32[]{:S(2)}, u32[]{:S(2)}) async-start(f32[32,32,128]{2,1,0:T(8,128)} %bitcast.7), calls=%async_computation.2 | async-start | bytes 1048576 | tf_op jit(solution)/shard_map/all_to_all | solution.py:10
  48.1 17.1 %all-to-all-done.2 = f32[32,32,128]{2,1,0:T(8,128)S(1)} async-done(((f32[32,32,128]{2,1,0:T(8,128)}), f32[32,32,128]{2,1,0:T(8,128)S(1)}, u32[]{:S(2)}, u32[]{:S(2)}) %all-to-all-start.2) | async-done | bytes 524320 | tf_op jit(solution)/shard_map/all_to_all | solution.py:10
  66.3 5.3 %all-to-all-start.3 = ((f32[32,2,32,128]{3,2,1,0:T(8,128)}), f32[32,2,32,128]{3,2,1,0:T(8,128)}, u32[]{:S(2)}, u32[]{:S(2)}) async-start(f32[32,2,32,128]{3,2,1,0:T(8,128)} %broadcast_in_dim.180), calls=%async_computation.3 | async-start | bytes 2097152 | tf_op jit(solution)/shard_map/all_to_all | solution.py:10
  76.4 23.9 %all-to-all-done.3 = f32[32,2,32,128]{3,2,1,0:T(8,128)} async-done(((f32[32,2,32,128]{3,2,1,0:T(8,128)}), f32[32,2,32,128]{3,2,1,0:T(8,128)}, u32[]{:S(2)}, u32[]{:S(2)}) %all-to-all-start.3) | async-done | bytes 1048608 | tf_op jit(solution)/shard_map/all_to_all | solution.py:10
  106.3 11.7 %cholesky.44 = f32[128,128]{1,0:T(8,128)S(1)} custom-call(f32[128,128]{1,0:T(8,128)S(1)} %fusion.34), custom_call_target="Cholesky" | custom-call | tf_op jit(solution)/shard_map/jit(cholesky)/cholesky | solution.py:19
  120.0 9.8 %custom-call.6 = f32[1,128,128]{1,2,0:T(8,128)S(1)} custom-call(f32[1,128,128]{2,1,0:T(8,128)S(1)} %get-tuple-element.43), custom_call_target="InvertDiagBlocksLowerTriangular" | custom-call | tf_op jit(solution)/shard_map/jit(_solve_triangular)/triangular_solve | solution.py:21
  133.7 11.9 %cholesky.55 = f32[128,128]{1,0:T(8,128)S(1)} custom-call(f32[128,128]{1,0:T(8,128)S(1)} %fusion.36), custom_call_target="Cholesky" | custom-call | tf_op jit(solution)/shard_map/jit(cholesky)/cholesky | solution.py:19
  147.0 9.8 %custom-call.7 = f32[1,128,128]{1,2,0:T(8,128)S(1)} custom-call(f32[1,128,128]{2,1,0:T(8,128)S(1)} %get-tuple-element.41), custom_call_target="InvertDiagBlocksLowerTriangular" | custom-call | tf_op jit(solution)/shard_map/jit(_solve_triangular)/triangular_solve | solution.py:21
  160.0 1.8 broadcast_select_fusion.1
  167.5 2.0 copy.106
  169.4 4.6 %fusion.8 = f32[768,3,128]{2,0,1:T(8,128)} fusion(f32[3,128,256]{2,1,0:T(8,128)} %bitcast.217, f32[1152,128]{0,1:T(8,128)S(1)} %copy-done.2, f32[1152,128]{0,1:T(8,128)S(1)} %get-tuple-element.56), kind=kOutput, calls=%fused_computation.24 | convolution fusion | flops 906166272 | bytes 2752512 | tf_op jit(solution)/shard_map/ab,jcb->ajc/dot_general | solution.py:84
  174.1 1.9 copy.103
  176.0 1.9 copy.105
  177.9 2.6 %fusion.3 = f32[768,3,128]{2,0,1:T(8,128)S(1)} fusion(f32[768,3,128]{2,0,1:T(8,128)} %fusion.8, f32[768,3,128]{2,0,1:T(8,128)S(1)} %bitcast.206, f32[768,128]{1,0:T(8,128)} %copy.105, f32[768,128]{1,0:T(8,128)} %copy.103, pred[3]{0:T(512)(128)(4,1)} %get-tuple-element.61, pred[3]{0:T(512)(128)(4,1)} %get-tuple-element.62, ...), kind=kOutput, calls=%fused_computation.7 | convolution fusion | flops 341250048 | bytes 4626176 | tf_op jit(solution)/shard_map/fr,fjc->rjc/dot_general | solution.py:87
  183.0 3.6 %all-to-all-start.4 = ((f32[16,8,128]{2,1,0:T(8,128)}), f32[16,8,128]{2,1,0:T(8,128)S(1)}, u32[]{:S(2)}, u32[]{:S(2)}) async-start(f32[16,8,128]{2,1,0:T(8,128)} %broadcast_in_dim.188), calls=%async_computation.4 | async-start | bytes 131072 | tf_op jit(solution)/shard_map/all_to_all | solution.py:10
  186.7 2.2 %copy.109 = f32[6,1,128,3,1,128]{5,4,3,2,1,0:T(1,128)} copy(f32[6,1,128,3,1,128]{5,2,0,3,4,1:T(8,128)S(1)} %bitcast.208) | data formatting | bytes 2359296
  188.9 3.8 %all-to-all-done.4 = f32[16,8,128]{2,1,0:T(8,128)S(1)} async-done(((f32[16,8,128]{2,1,0:T(8,128)}), f32[16,8,128]{2,1,0:T(8,128)S(1)}, u32[]{:S(2)}, u32[]{:S(2)}) %all-to-all-start.4) | async-done | bytes 65568 | tf_op jit(solution)/shard_map/all_to_all | solution.py:10
  193.5 7.6 %all-to-all-start.5 = ((f32[32,14,128]{2,1,0:T(8,128)}), f32[32,14,128]{2,1,0:T(8,128)S(1)}, u32[]{:S(2)}, u32[]{:S(2)}) async-start(f32[32,14,128]{2,1,0:T(8,128)} %broadcast_in_dim.196), calls=%async_computation.5 | async-start | bytes 524288 | tf_op jit(solution)/shard_map/all_to_all | solution.py:10
  203.5 12.2 %all-to-all-done.5 = f32[32,14,128]{2,1,0:T(8,128)S(1)} async-done(((f32[32,14,128]{2,1,0:T(8,128)}), f32[32,14,128]{2,1,0:T(8,128)S(1)}, u32[]{:S(2)}, u32[]{:S(2)}) %all-to-all-start.5) | async-done | bytes 229408 | tf_op jit(solution)/shard_map/all_to_all | solution.py:10
  (147 shorter events, 41.3 us)
Async XLA Ops:
  0.6 19.7 %copy-start.8 = (f32[6,1,128,3,1,128]{5,4,3,2,1,0:T(1,128)S(1)}, f32[6,1,128,3,1,128]{5,4,3,2,1,0:T(1,128)}, u32[]{:S(2)}) copy-start(f32[6,1,128,3,1,128]{5,4,3,2,1,0:T(1,128)} %param.9) | copy-start | bytes 3538948
  2.4 13.6 %all-to-all-start = ((f32[16,24,128]{2,1,0:T(8,128)}), f32[16,24,128]{2,1,0:T(8,128)S(1)}, u32[]{:S(2)}, u32[]{:S(2)}) async-start(f32[16,24,128]{2,1,0:T(8,128)} %bitcast.2), calls=%async_computation | async-start | bytes 393216 | tf_op jit(solution)/shard_map/all_to_all | solution.py:10
  16.8 13.0 %all-to-all-start.1 = ((f32[16,2,24,128]{3,2,1,0:T(8,128)}), f32[16,2,24,128]{3,2,1,0:T(8,128)S(1)}, u32[]{:S(2)}, u32[]{:S(2)}) async-start(f32[16,2,24,128]{3,2,1,0:T(8,128)} %broadcast_in_dim.179), calls=%async_computation.1 | async-start | bytes 786432 | tf_op jit(solution)/shard_map/all_to_all | solution.py:10
  30.0 18.1 %copy-start.28 = (s32[96]{0:T(128)S(1)}, s32[96]{0:T(128)}, u32[]{:S(2)}) copy-start(s32[96]{0:T(128)} %param.14) | copy-start | bytes 1156
  30.0 18.1 %copy-start.13 = (s32[3,1,128]{2,1,0:T(1,128)S(1)}, s32[3,1,128]{2,1,0:T(1,128)}, u32[]{:S(2)}) copy-start(s32[3,1,128]{2,1,0:T(1,128)} %param.11) | copy-start | bytes 4612
  30.9 34.3 %all-to-all-start.2 = ((f32[32,32,128]{2,1,0:T(8,128)}), f32[32,32,128]{2,1,0:T(8,128)S(1)}, u32[]{:S(2)}, u32[]{:S(2)}) async-start(f32[32,32,128]{2,1,0:T(8,128)} %bitcast.7), calls=%async_computation.2 | async-start | bytes 1048576 | tf_op jit(solution)/shard_map/all_to_all | solution.py:10
  66.3 6.9 %copy-start.24 = (s32[96,2]{0,1:T(2,128)S(1)}, s32[96,2]{0,1:T(2,128)}, u32[]{:S(2)}) copy-start(s32[96,2]{0,1:T(2,128)} %param.13) | copy-start | bytes 2308
  66.3 6.9 %copy-start.25 = (s32[96,2]{0,1:T(2,128)S(1)}, s32[96,2]{0,1:T(2,128)}, u32[]{:S(2)}) copy-start(s32[96,2]{0,1:T(2,128)} %param.12) | copy-start | bytes 2308
  66.3 34.0 %all-to-all-start.3 = ((f32[32,2,32,128]{3,2,1,0:T(8,128)}), f32[32,2,32,128]{3,2,1,0:T(8,128)}, u32[]{:S(2)}, u32[]{:S(2)}) async-start(f32[32,2,32,128]{3,2,1,0:T(8,128)} %broadcast_in_dim.180), calls=%async_computation.3 | async-start | bytes 2097152 | tf_op jit(solution)/shard_map/all_to_all | solution.py:10
  73.2 2.0 copy-start.18
  74.2 2.2 %copy-start = (f32[2,1408,128]{1,2,0:T(8,128)}, f32[2,1408,128]{1,2,0:T(8,128)S(1)}, u32[]{:S(2)}) copy-start(f32[2,1408,128]{1,2,0:T(8,128)S(1)} %convolution_bitcast_fusion) | copy-start | bytes 4325380
  158.0 2.0 copy-start.4
  161.8 4.9 %copy-start.1 = (f32[1152,128]{0,1:T(8,128)}, f32[1152,128]{0,1:T(8,128)S(1)}, u32[]{:S(2)}) copy-start(f32[1152,128]{0,1:T(8,128)S(1)} %get-tuple-element.39) | copy-start | bytes 1769476
  180.5 6.0 %copy-start.22 = (f32[1,128]{1,0:T(1,128)S(1)}, f32[1,128]{1,0:T(1,128)}, u32[]{:S(2)}) copy-start(f32[1,128]{1,0:T(1,128)} %fusion.19) | copy-start | bytes 1540
  180.6 6.0 %copy-start.23 = (f32[1,128]{1,0:T(1,128)S(1)}, f32[1,128]{1,0:T(1,128)}, u32[]{:S(2)}) copy-start(f32[1,128]{1,0:T(1,128)} %fusion.22) | copy-start | bytes 1540
  180.6 6.0 %copy-start.26 = (pred[2]{0:T(512)(128)(4,1)S(1)}, pred[2]{0:T(512)(128)(4,1)}, u32[]{:S(2)}) copy-start(pred[2]{0:T(512)(128)(4,1)} %iota_compare_fusion.4) | copy-start | bytes 10
  180.6 6.0 %copy-start.27 = (f32[128]{0:T(128)S(1)}, f32[128]{0:T(128)}, u32[]{:S(2)}) copy-start(f32[128]{0:T(128)} %slice_bitcast_fusion.11) | copy-start | bytes 1540
  183.0 9.7 %all-to-all-start.4 = ((f32[16,8,128]{2,1,0:T(8,128)}), f32[16,8,128]{2,1,0:T(8,128)S(1)}, u32[]{:S(2)}, u32[]{:S(2)}) async-start(f32[16,8,128]{2,1,0:T(8,128)} %broadcast_in_dim.188), calls=%async_computation.4 | async-start | bytes 131072 | tf_op jit(solution)/shard_map/all_to_all | solution.py:10
  186.7 14.4 %copy-start.10 = (f32[128,128]{1,0:T(8,128)S(1)}, f32[128,128]{1,0:T(8,128)}, u32[]{:S(2)}) copy-start(f32[128,128]{1,0:T(8,128)} %copy-done.9) | copy-start | bytes 196612
  186.7 14.5 %copy-start.7 = (f32[128,128]{1,0:T(8,128)S(1)}, f32[128,128]{1,0:T(8,128)}, u32[]{:S(2)}) copy-start(f32[128,128]{1,0:T(8,128)} %copy-done.5) | copy-start | bytes 196612
  186.7 14.8 %copy-start.12 = (f32[128,128]{1,0:T(8,128)S(1)}, f32[128,128]{1,0:T(8,128)}, u32[]{:S(2)}) copy-start(f32[128,128]{1,0:T(8,128)} %fusion.27) | copy-start | bytes 196612
  188.9 13.3 %copy-start.20 = (pred[3]{0:T(512)(128)(4,1)S(1)}, pred[3]{0:T(512)(128)(4,1)}, u32[]{:S(2)}) copy-start(pred[3]{0:T(512)(128)(4,1)} %get-tuple-element.61) | copy-start | bytes 13
  188.9 13.3 %copy-start.21 = (pred[3]{0:T(512)(128)(4,1)S(1)}, pred[3]{0:T(512)(128)(4,1)}, u32[]{:S(2)}) copy-start(pred[3]{0:T(512)(128)(4,1)} %get-tuple-element.62) | copy-start | bytes 13
  193.5 22.3 %all-to-all-start.5 = ((f32[32,14,128]{2,1,0:T(8,128)}), f32[32,14,128]{2,1,0:T(8,128)S(1)}, u32[]{:S(2)}, u32[]{:S(2)}) async-start(f32[32,14,128]{2,1,0:T(8,128)} %broadcast_in_dim.196), calls=%async_computation.5 | async-start | bytes 524288 | tf_op jit(solution)/shard_map/all_to_all | solution.py:10
  (11 other events, 13.9 us)
